TPU v7x, 32 devices: a whole 2x2x4 slice. The times are simulated.
32 devices in a mesh: row: 8 (over y, x, core), col: 4 (over z).
Axes of the slice: x: 2, y: 2, z: 4, core: 2. Of those that a mesh axis runs over, the one named last changes fastest.
Arguments:
- upper_s: float32 [4, 2048, 8, 1024], P(None, 'row', None, 'col')
- upper_t: float32 [4, 2048, 8, 1024], P(None, 'row', None, 'col')
- left_vectors: float32 [4, 2048, 8, 1024], P(None, 'row', None, 'col'), may hold values from -6 to 6
- right_vectors: float32 [4, 2048, 8, 1024], P(None, 'row', None, 'col'), may hold values from -6 to 6
- window_starts: int32 [3, 16], replicated, may hold values from 0 to 31, as said below
- selection: int32 [3, 16, 256], replicated, may hold values 0 or 1
- window_factors: float32 [3, 16, 2, 256, 256], P(None, 'row')
Outputs:
- new_s: float32 [4, 2048, 8, 1024], P(None, 'row', None, 'col')
- new_t: float32 [4, 2048, 8, 1024], P(None, 'row', None, 'col')
- new_left: float32 [4, 2048, 8, 1024], P(None, 'row', None, 'col')
- new_right: float32 [4, 2048, 8, 1024], P(None, 'row', None, 'col')
Inputs may be any that keep to these rules, and one draw needn't show every extreme that they name: `window_starts`: within each round the 16 block numbers are distinct.
All inputs are finite; a program needn't handle non-finite values.
Results may differ from a plain program's by a relative error of at most 0.0001.
Values sent between devices are 32-bit elements; how exact they have to be, the bound alone decides.
No kernel may reach another device: no remote copies, remote signals or barrier semaphores. Data moves between devices by JAX's collectives and lax.ppermute only.
A program may use at most 192 MiB of HBM per device.

v0:
```python
import jax
import jax.numpy as jnp
from jax import lax
from jax.sharding import PartitionSpec as P


def destinations(flags):
    earlier = jnp.cumsum(flags) - flags
    chosen = jnp.sum(flags)
    position = jnp.arange(flags.shape[0], dtype=jnp.int32)
    return jnp.where(flags == 1, earlier, chosen + position - earlier)


def window_bases(factors, flags):
    target = destinations(flags)
    return (jnp.take(factors[0], target, axis=0), jnp.take(factors[1], target, axis=0))


def fill_identity(starts, blocks, chosen):
    covered = jnp.sum((blocks[:, None] == starts[None, :]).astype(jnp.float32), axis=1)
    order_w = chosen.shape[1]
    return chosen + (1.0 - covered)[:, None, None] * jnp.eye(order_w, dtype=jnp.float32)


def rows_update(factor, matrix):
    return jnp.einsum("aij,aibl->ajbl", factor, matrix, precision=lax.Precision.HIGHEST)


def cols_update(matrix, factor):
    return jnp.einsum("aibm,bml->aibl", matrix, factor, precision=lax.Precision.HIGHEST)


def slot_factors(own_factors, own_starts, own_flags, starts, row_blocks, col_blocks):
    left_own, right_own = jax.vmap(window_bases)(own_factors, own_flags)
    stacked = jnp.stack([left_own, right_own], axis=1)
    placing = (col_blocks[:, None] == own_starts[None, :]).astype(jnp.float32)
    slots = jnp.einsum("jw,wxab->jxab", placing, stacked, precision=lax.Precision.HIGHEST)
    received = lax.psum(slots, "row")
    picking = (row_blocks[:, None] == col_blocks[None, :]).astype(jnp.float32)
    row_part = jnp.einsum("kj,jab->kab", picking, received[:, 0], precision=lax.Precision.HIGHEST)
    row_sum = lax.psum(row_part, "col")
    left_rows = fill_identity(starts, row_blocks, row_sum)
    left_cols = fill_identity(starts, col_blocks, received[:, 0])
    right_cols = fill_identity(starts, col_blocks, received[:, 1])
    return (left_rows, left_cols, right_cols)


def shards(upper_s, upper_t, left_vectors, right_vectors, window_starts, selection, window_factors):
    row_index = lax.axis_index("row")
    col_index = lax.axis_index("col")
    row_count = lax.axis_size("row")
    col_count = lax.axis_size("col")
    local_rows = upper_s.shape[0]
    local_cols = upper_s.shape[2]
    round_count = window_starts.shape[0]
    own_count = window_factors.shape[1]
    row_blocks = jnp.arange(local_rows, dtype=jnp.int32) * row_count + row_index
    col_blocks = jnp.arange(local_cols, dtype=jnp.int32) * col_count + col_index
    for round_idx in range(round_count):
        starts = window_starts[round_idx]
        first = row_index * own_count
        own_starts = lax.dynamic_slice_in_dim(starts, first, own_count, 0)
        own_flags = lax.dynamic_slice_in_dim(selection[round_idx], first, own_count, 0)
        left_rows, left_cols, right_cols = slot_factors(
            window_factors[round_idx], own_starts, own_flags, starts, row_blocks, col_blocks
        )
        upper_s = cols_update(rows_update(left_rows, upper_s), right_cols)
        upper_t = cols_update(rows_update(left_rows, upper_t), right_cols)
        left_vectors = cols_update(left_vectors, left_cols)
        right_vectors = cols_update(right_vectors, right_cols)
    return (upper_s, upper_t, left_vectors, right_vectors)


def solution(mesh):
    return jax.shard_map(
        shards,
        mesh=mesh,
        in_specs=(
            P(None, "row", None, "col"),
            P(None, "row", None, "col"),
            P(None, "row", None, "col"),
            P(None, "row", None, "col"),
            P(),
            P(),
            P(None, "row", None, None, None),
        ),
        out_specs=(
            P(None, "row", None, "col"),
            P(None, "row", None, "col"),
            P(None, "row", None, "col"),
            P(None, "row", None, "col"),
        ),
        check_vma=False,
    )
```

profile of v0, /device:TPU:0, one launch (start us, length us, event | category | flops | bytes accessed | tf_op | source)
XLA Modules:
  0.0 584.6 jit_solution(2492521393092527794)
XLA Ops:
  12.0 6.4 %gather_fusion = f32[512,256]{1,0:T(8,128)} fusion(f32[2,256,256]{2,1,0:T(8,128)S(1)} %get-tuple-element.58, s32[512]{0:T(512)S(1)} %bitcast.239), kind=kCustom, calls=%fused_computation.clone | custom fusion | bytes 1052672 | tf_op jit(solution)/shard_map/vmap(jit(_take))/gather | solution.py:16
  18.4 6.4 %gather_fusion.1 = f32[512,256]{1,0:T(8,128)} fusion(f32[2,256,256]{2,1,0:T(8,128)S(1)} %get-tuple-element.59, s32[512]{0:T(512)S(1)} %bitcast.240), kind=kCustom, calls=%fused_computation.1.clone | custom fusion | bytes 1052672 | tf_op jit(solution)/shard_map/vmap(jit(_take))/gather | solution.py:16
  29.0 6.4 %gather_fusion.2 = f32[512,256]{1,0:T(8,128)} fusion(f32[2,256,256]{2,1,0:T(8,128)S(1)} %get-tuple-element.56, s32[512]{0:T(512)S(1)} %bitcast.243), kind=kCustom, calls=%fused_computation.2.clone | custom fusion | bytes 1052672 | tf_op jit(solution)/shard_map/vmap(jit(_take))/gather | solution.py:16
  35.3 6.4 %gather_fusion.3 = f32[512,256]{1,0:T(8,128)} fusion(f32[2,256,256]{2,1,0:T(8,128)S(1)} %get-tuple-element.57, s32[512]{0:T(512)S(1)} %bitcast.244), kind=kCustom, calls=%fused_computation.3.clone | custom fusion | bytes 1052672 | tf_op jit(solution)/shard_map/vmap(jit(_take))/gather | solution.py:16
  54.1 4.3 fusion.42
  58.4 4.3 fusion.46
  63.9 15.0 %fusion.50 = f32[8,2,256,256]{3,0,2,1:T(8,128)} fusion(f32[2,1,256,256]{3,0,2,1:T(2,128)S(1)} %get-tuple-element.68, f32[2,1,256,256]{3,0,2,1:T(2,128)S(1)} %get-tuple-element.67, s32[8]{0:T(128)S(1)} %multiply_add_fusion.16, s32[2]{0:T(128)S(1)} %fusion.102), kind=kOutput, calls=%fused_computation.66 | convolution fusion | flops 25427984 | bytes 5242920 | tf_op jit(solution)/shard_map/jw,wxab->jxab/dot_general | solution.py:37
  79.4 174.4 %all-reduce.5.cloned.1.call-done = (f32[8,2,256,256]{3,0,2,1:T(8,128)}, f32[8,2,256,256]{3,0,2,1:T(8,128)}, f32[8,2,256,256]{3,0,2,1:T(8,128)}) async-done(((f32[8,2,256,256]{3,0,2,1:T(8,128)}, f32[8,2,256,256]{3,0,2,1:T(8,128)}, f32[8,2,256,256]{3,0,2,1:T(8,128)}), (f32[8,2,256,256]{3,0,2,1:T(8,128)}, f32[8,2,256,256]{3,0,2,1:T(8,128)}, f32[8,2,256,256]{3,0,2,1:T(8,128)})) %all-reduce.5.cloned.1.call-update) | async-done | bytes 12582928 | tf_op jit(solution)/shard_map/psum | solution.py:38
  264.0 8.5 %fusion.31 = (f32[8,256,256,1]{2,0,1,3:T(8,128)}, f32[8,256,256,1]{2,0,1,3:T(8,128)}, f32[8,256,256,1]{2,0,1,3:T(8,128)}, f32[8,256,256,1]{2,0,1,3:T(8,128)S(1)}...) fusion(f32[8,2,256,256]{3,0,2,1:T(8,128)} %get-tuple-element.27, f32[256,256]{1,0:T(8,128)S(1)} %fusion.78, ...), kind=kLoop, calls=%fused_computation.41 | loop fusion | flops 4718592 | bytes 25428064 | tf_op jit(solution)/shard_map/add | solution.py:22
  272.5 21.2 %fusion.22 = f32[8,256,4,256]{3,1,2,0:T(8,128)} fusion(f32[4,256,8,256]{3,2,1,0:T(8,128)} %param.11, f32[8,256,256,1]{2,0,1,3:T(8,128)S(1)} %get-tuple-element.61), kind=kOutput, calls=%fused_computation.28 | convolution fusion | flops 6442450944 | bytes 18874368 | tf_op jit(solution)/shard_map/aibm,bml->aibl/dot_general | solution.py:30
  293.8 12.7 %fusion.6 = f32[8,256,4,256]{3,1,2,0:T(8,128)} fusion(f32[8,256,4,256]{3,1,2,0:T(8,128)} %fusion.22, f32[8,256,256,1]{2,0,1,3:T(8,128)S(1)} %get-tuple-element.63), kind=kOutput, calls=%fused_computation.12 | convolution fusion | flops 6442450944 | bytes 18874368 | tf_op jit(solution)/shard_map/aibm,bml->aibl/dot_general | solution.py:30
  314.3 15.9 %fusion.24 = f32[4,256,8,256]{1,3,0,2:T(8,128)} fusion(f32[8,256,4,256]{3,1,2,0:T(8,128)} %fusion.6, f32[8,256,256,1]{2,0,1,3:T(8,128)} %get-tuple-element.45), kind=kOutput, calls=%fused_computation.30 | convolution fusion | flops 6442450944 | bytes 18874368 | tf_op jit(solution)/shard_map/aibm,bml->aibl/dot_general | solution.py:30
  330.1 10.4 %copy.155 = f32[4,256,8,256]{3,2,1,0:T(8,128)} copy(f32[4,256,8,256]{1,3,0,2:T(8,128)} %fusion.24) | data formatting | bytes 16777216
  340.5 14.8 %fusion.20 = f32[8,256,4,256]{3,1,2,0:T(8,128)S(1)} fusion(f32[8,256,256,1]{1,2,3,0:T(8,128)} %copy.163, f32[4,256,8,256]{3,2,1,0:T(8,128)} %param.12), kind=kOutput, calls=%fused_computation.26 | convolution fusion | flops 6442450944 | bytes 18874368 | tf_op jit(solution)/shard_map/aibm,bml->aibl/dot_general | solution.py:30
  355.4 8.8 %fusion.2 = f32[8,256,4,256]{3,1,2,0:T(8,128)S(1)} fusion(f32[8,256,256,1]{1,2,3,0:T(8,128)S(1)} %copy-done, f32[8,256,4,256]{3,1,2,0:T(8,128)S(1)} %fusion.20), kind=kOutput, calls=%fused_computation.8 | convolution fusion | flops 6442450944 | bytes 18874368 | tf_op jit(solution)/shard_map/aibm,bml->aibl/dot_general | solution.py:30
  364.2 9.8 %fusion.27 = f32[4,256,8,256]{1,3,0,2:T(8,128)} fusion(f32[8,256,256,1]{1,2,3,0:T(8,128)S(1)} %copy.170, f32[8,256,4,256]{3,1,2,0:T(8,128)S(1)} %fusion.2), kind=kOutput, calls=%fused_computation.31 | convolution fusion | flops 6442450944 | bytes 18874368 | tf_op jit(solution)/shard_map/aibm,bml->aibl/dot_general | solution.py:30
  374.0 10.4 %copy.156 = f32[4,256,8,256]{3,2,1,0:T(8,128)} copy(f32[4,256,8,256]{1,3,0,2:T(8,128)} %fusion.27) | data formatting | bytes 16777216
  384.4 30.7 %all-reduce.7.cloned.1.call-done = (f32[4,256,256]{2,1,0:T(8,128)}, f32[4,256,256]{2,1,0:T(8,128)}, f32[4,256,256]{2,1,0:T(8,128)}) async-done(((f32[4,256,256]{2,1,0:T(8,128)}, f32[4,256,256]{2,1,0:T(8,128)}, f32[4,256,256]{2,1,0:T(8,128)}), (f32[4,256,256]{2,1,0:T(8,128)}, f32[4,256,256]{2,1,0:T(8,128)}, f32[4,256,256]{2,1,0:T(8,128)})) %all-reduce.7.cloned.1.call-update) | async-done | bytes 3145744 | tf_op jit(solution)/shard_map/psum | solution.py:41
  415.1 14.4 %fusion.18 = f32[4,256,8,256]{3,1,0,2:T(8,128)S(1)} fusion(f32[4,256,8,256]{3,2,1,0:T(8,128)} %param.9, f32[4,256,256]{2,1,0:T(8,128)} %get-tuple-element.30, f32[4]{0:T(128)S(1)} %get-tuple-element.87, f32[256,256]{1,0:T(8,128)S(1)} %fusion.78), kind=kOutput, calls=%fused_computation.24 | convolution fusion | flops 6442975232 | bytes 18087952 | tf_op jit(solution)/shard_map/aij,aibl->ajbl/dot_general | solution.py:26
  429.5 8.9 %fusion.117 = f32[8,256,4,256]{3,1,2,0:T(8,128)S(1)} fusion(f32[8,256,256,1]{1,2,3,0:T(8,128)S(1)} %copy-done.3, f32[4,256,8,256]{3,1,0,2:T(8,128)S(1)} %fusion.18), kind=kOutput, calls=%fused_computation.194 | convolution fusion | flops 6442450944 | bytes 18874368 | tf_op jit(solution)/shard_map/aibm,bml->aibl/dot_general | solution.py:30
  438.4 14.3 %fusion.16 = f32[4,256,8,256]{3,1,0,2:T(8,128)S(1)} fusion(f32[8,256,4,256]{3,1,2,0:T(8,128)S(1)} %fusion.117, f32[4,256,256]{2,1,0:T(8,128)S(1)} %copy-done.7, f32[4]{0:T(128)S(1)} %get-tuple-element.88, f32[256,256]{1,0:T(8,128)S(1)} %fusion.78), kind=kOutput, calls=%fused_computation.22 | convolution fusion | flops 6442975232 | bytes 18087952 | tf_op jit(solution)/shard_map/aij,aibl->ajbl/dot_general | solution.py:26
  452.7 9.3 %fusion.118 = f32[8,256,4,256]{3,1,2,0:T(8,128)S(1)} fusion(f32[8,256,256,1]{1,2,3,0:T(8,128)S(1)} %copy-done.1, f32[4,256,8,256]{3,1,0,2:T(8,128)S(1)} %fusion.16), kind=kOutput, calls=%fused_computation.195 | convolution fusion | flops 6442450944 | bytes 18874368 | tf_op jit(solution)/shard_map/aibm,bml->aibl/dot_general | solution.py:30
  462.0 14.2 %fusion.14 = f32[4,256,8,256]{3,1,0,2:T(8,128)S(1)} fusion(f32[8,256,4,256]{3,1,2,0:T(8,128)S(1)} %fusion.118, f32[4,256,256]{2,1,0:T(8,128)S(1)} %copy-done.6, f32[256,256]{1,0:T(8,128)S(1)} %fusion.78, f32[4]{0:T(128)S(1)} %broadcast_subtract_fusion.2), kind=kOutput, calls=%fused_computation.20 | convolution fusion | flops 6442975232 | bytes 18087952 | tf_op jit(solution)/shard_map/aij,aibl->ajbl/dot_general | solution.py:26
  476.3 9.7 %convolution_bitcast_fusion.1 = f32[4,256,8,256]{1,3,0,2:T(8,128)} fusion(f32[8,256,256,1]{1,2,3,0:T(8,128)S(1)} %copy.170, f32[4,256,8,256]{3,1,0,2:T(8,128)S(1)} %fusion.14), kind=kOutput, calls=%fused_computation.33 | convolution fusion | flops 6442450944 | bytes 18874368 | tf_op jit(solution)/shard_map/aibm,bml->aibl/dot_general | solution.py:30
  486.0 10.4 %copy.153 = f32[4,256,8,256]{3,2,1,0:T(8,128)} copy(f32[4,256,8,256]{1,3,0,2:T(8,128)} %convolution_bitcast_fusion.1) | data formatting | bytes 16777216
  496.4 14.4 %fusion.12 = f32[4,256,8,256]{3,1,0,2:T(8,128)S(1)} fusion(f32[4,256,8,256]{3,2,1,0:T(8,128)} %param.10, f32[4,256,256]{2,1,0:T(8,128)} %get-tuple-element.30, f32[4]{0:T(128)S(1)} %get-tuple-element.87, f32[256,256]{1,0:T(8,128)S(1)} %fusion.78), kind=kOutput, calls=%fused_computation.18 | convolution fusion | flops 6442975232 | bytes 18087952 | tf_op jit(solution)/shard_map/aij,aibl->ajbl/dot_general | solution.py:26
  510.8 8.9 %fusion.119 = f32[8,256,4,256]{3,1,2,0:T(8,128)S(1)} fusion(f32[8,256,256,1]{1,2,3,0:T(8,128)S(1)} %copy-done.4, f32[4,256,8,256]{3,1,0,2:T(8,128)S(1)} %fusion.12), kind=kOutput, calls=%fused_computation.196 | convolution fusion | flops 6442450944 | bytes 18874368 | tf_op jit(solution)/shard_map/aibm,bml->aibl/dot_general | solution.py:30
  519.7 14.3 %fusion.10 = f32[4,256,8,256]{3,1,0,2:T(8,128)S(1)} fusion(f32[8,256,4,256]{3,1,2,0:T(8,128)S(1)} %fusion.119, f32[4,256,256]{2,1,0:T(8,128)S(1)} %copy-done.8, f32[4]{0:T(128)S(1)} %get-tuple-element.88, f32[256,256]{1,0:T(8,128)S(1)} %fusion.78), kind=kOutput, calls=%fused_computation.16 | convolution fusion | flops 6442975232 | bytes 18087952 | tf_op jit(solution)/shard_map/aij,aibl->ajbl/dot_general | solution.py:26
  534.0 9.3 %fusion.120 = f32[8,256,4,256]{3,1,2,0:T(8,128)S(1)} fusion(f32[8,256,256,1]{1,2,3,0:T(8,128)S(1)} %copy-done.2, f32[4,256,8,256]{3,1,0,2:T(8,128)S(1)} %fusion.10), kind=kOutput, calls=%fused_computation.197 | convolution fusion | flops 6442450944 | bytes 18874368 | tf_op jit(solution)/shard_map/aibm,bml->aibl/dot_general | solution.py:30
  543.3 14.2 %fusion.8 = f32[4,256,8,256]{3,1,0,2:T(8,128)S(1)} fusion(f32[8,256,4,256]{3,1,2,0:T(8,128)S(1)} %fusion.120, f32[4,256,256]{2,1,0:T(8,128)S(1)} %copy-done.6, f32[256,256]{1,0:T(8,128)S(1)} %fusion.78, f32[4]{0:T(128)S(1)} %broadcast_subtract_fusion.2), kind=kOutput, calls=%fused_computation.14 | convolution fusion | flops 6442975232 | bytes 18087952 | tf_op jit(solution)/shard_map/aij,aibl->ajbl/dot_general | solution.py:26
  557.5 9.7 %convolution_bitcast_fusion = f32[4,256,8,256]{1,3,0,2:T(8,128)} fusion(f32[8,256,256,1]{1,2,3,0:T(8,128)S(1)} %copy.170, f32[4,256,8,256]{3,1,0,2:T(8,128)S(1)} %fusion.8), kind=kOutput, calls=%fused_computation.32 | convolution fusion | flops 6442450944 | bytes 18874368 | tf_op jit(solution)/shard_map/aibm,bml->aibl/dot_general | solution.py:30
  567.2 10.4 %copy.154 = f32[4,256,8,256]{3,2,1,0:T(8,128)} copy(f32[4,256,8,256]{1,3,0,2:T(8,128)} %convolution_bitcast_fusion) | data formatting | bytes 16777216
  (94 shorter events, 40.9 us)
Async XLA Ops:
  7.2 3.3 copy-start.12
  7.2 246.6 %all-reduce.5.cloned.1.call-start = ((), (), s32[]{:S(2)}) async-start(), calls=%async_computation | async-start | bytes 25165824 | tf_op jit(solution)/shard_map/psum | solution.py:38
  10.3 14.5 %copy-start.13 = (s32[3,16]{1,0:T(4,128)S(1)}, s32[3,16]{1,0:T(4,128)}, u32[]{:S(2)}) copy-start(s32[3,16]{1,0:T(4,128)} %param.13) | copy-start | bytes 580
  35.3 14.7 %copy-start.9 = (f32[512,256]{1,0:T(8,128)S(1)}, f32[512,256]{1,0:T(8,128)}, u32[]{:S(2)}) copy-start(f32[512,256]{1,0:T(8,128)} %gather_fusion) | copy-start | bytes 1572868
  35.3 14.7 %copy-start.10 = (f32[512,256]{1,0:T(8,128)S(1)}, f32[512,256]{1,0:T(8,128)}, u32[]{:S(2)}) copy-start(f32[512,256]{1,0:T(8,128)} %gather_fusion.1) | copy-start | bytes 1572868
  41.8 9.4 %copy-start.11 = (f32[512,256]{1,0:T(8,128)S(1)}, f32[512,256]{1,0:T(8,128)}, u32[]{:S(2)}) copy-start(f32[512,256]{1,0:T(8,128)} %gather_fusion.3) | copy-start | bytes 1572868
  78.9 336.2 %all-reduce.7.cloned.1.call-start = ((), (), s32[]{:S(2)}) async-start(), calls=%async_computation.1 | async-start | bytes 6291456 | tf_op jit(solution)/shard_map/psum | solution.py:41
  253.8 7.9 %copy-start.5 = (f32[8,2,256,256]{3,0,2,1:T(8,128)S(1)}, f32[8,2,256,256]{3,0,2,1:T(8,128)}, u32[]{:S(2)}) copy-start(f32[8,2,256,256]{3,0,2,1:T(8,128)} %get-tuple-element.27) | copy-start | bytes 12582916
  340.5 14.8 %copy-start = (f32[8,256,256,1]{1,2,3,0:T(8,128)S(1)}, f32[8,256,256,1]{1,2,3,0:T(8,128)}, u32[]{:S(2)}) copy-start(f32[8,256,256,1]{1,2,3,0:T(8,128)} %copy.167) | copy-start | bytes 6291460
  415.1 14.4 %copy-start.3 = (f32[8,256,256,1]{1,2,3,0:T(8,128)S(1)}, f32[8,256,256,1]{1,2,3,0:T(8,128)}, u32[]{:S(2)}) copy-start(f32[8,256,256,1]{1,2,3,0:T(8,128)} %copy.163) | copy-start | bytes 6291460
  429.5 8.9 %copy-start.7 = (f32[4,256,256]{2,1,0:T(8,128)S(1)}, f32[4,256,256]{2,1,0:T(8,128)}, u32[]{:S(2)}) copy-start(f32[4,256,256]{2,1,0:T(8,128)} %get-tuple-element.31) | copy-start | bytes 3145732
  438.4 14.3 %copy-start.1 = (f32[8,256,256,1]{1,2,3,0:T(8,128)S(1)}, f32[8,256,256,1]{1,2,3,0:T(8,128)}, u32[]{:S(2)}) copy-start(f32[8,256,256,1]{1,2,3,0:T(8,128)} %copy.167) | copy-start | bytes 6291460
  452.7 9.3 %copy-start.6 = (f32[4,256,256]{2,1,0:T(8,128)S(1)}, f32[4,256,256]{2,1,0:T(8,128)}, u32[]{:S(2)}) copy-start(f32[4,256,256]{2,1,0:T(8,128)} %get-tuple-element.32) | copy-start | bytes 3145732
  496.4 14.4 %copy-start.4 = (f32[8,256,256,1]{1,2,3,0:T(8,128)S(1)}, f32[8,256,256,1]{1,2,3,0:T(8,128)}, u32[]{:S(2)}) copy-start(f32[8,256,256,1]{1,2,3,0:T(8,128)} %copy.163) | copy-start | bytes 6291460
  510.8 8.9 %copy-start.8 = (f32[4,256,256]{2,1,0:T(8,128)S(1)}, f32[4,256,256]{2,1,0:T(8,128)}, u32[]{:S(2)}) copy-start(f32[4,256,256]{2,1,0:T(8,128)} %get-tuple-element.31) | copy-start | bytes 3145732
  519.7 14.3 %copy-start.2 = (f32[8,256,256,1]{1,2,3,0:T(8,128)S(1)}, f32[8,256,256,1]{1,2,3,0:T(8,128)}, u32[]{:S(2)}) copy-start(f32[8,256,256,1]{1,2,3,0:T(8,128)} %copy.167) | copy-start | bytes 6291460
Sparse Core Ops, SparseCore 0:
  79.0 174.7 all-reduce.4
  293.9 121.1 all-reduce.6
where the time goes:
time: 594 us; the launch traced here: 585 us
  matrix products  255 us (43%)
  waiting for transfers between devices  205 us (35%)
  local copies, waits for them, and re-layouts  92.4 us (16%)
  other arithmetic  17.4 us (3%)
  between operations  14.7 us (2%)
    psum x1, waiting for transfers between devices, slot_factors(): received = lax.psum(slots, 'row')  174 us
    dot_general x12, matrix products, cols_update(): jnp.einsum('aibm,bml->aibl', matrix, factor, precision=lax.Precision.HIGH...  139 us
    dot_general x6, matrix products, rows_update(): jnp.einsum('aij,aibl->ajbl', factor, matrix, precision=lax.Precision.HIGH...  85.8 us
    unnamed x36, local copies, waits for them, and re-layouts  41.7 us
    psum x1, waiting for transfers between devices, slot_factors(): row_sum = lax.psum(row_part, 'col')  30.7 us
    dot_general x3, matrix products, slot_factors(): jnp.einsum('jw,wxab->jxab', placing, stacked, precision=lax.Precision.HIG...  23.5 us
    gather x3, local copies, waits for them, and re-layouts, window_bases(): jnp.take(factors[0], target, axis=0)  16.7 us
    gather x3, local copies, waits for them, and re-layouts, window_bases(): jnp.take(factors[1], target, axis=0)  16.6 us
  transfers between devices with their start and end apart: 2, of which 2 were waited for; matrix products, arithmetic and copies ran while one was open for 16% of the time, Pallas kernels for 0%

commit v1 on v0

--- a/solution.py
+++ b/solution.py
@@ -38,7 +38,7 @@
     received = lax.psum(slots, "row")
     picking = (row_blocks[:, None] == col_blocks[None, :]).astype(jnp.float32)
     row_part = jnp.einsum("kj,jab->kab", picking, received[:, 0], precision=lax.Precision.HIGHEST)
-    row_sum = lax.psum(row_part, "col")
+    row_sum = jnp.sum(lax.all_gather(row_part, "col"), axis=0)
     left_rows = fill_identity(starts, row_blocks, row_sum)
     left_cols = fill_identity(starts, col_blocks, received[:, 0])
     right_cols = fill_identity(starts, col_blocks, received[:, 1])

time: 594 us -> 628 us (1.057)
  waiting for transfers between devices: 205 us -> 239 us
  matrix products: 255 us -> 244 us
  other arithmetic: 17.4 us -> 27.9 us
    all_gather x0 -> x3, waiting for transfers between devices: none -> 64.3 us  [slot_factors(): row_sum = jnp.sum(lax.all_gather(row_part, 'col'), axis=0)]
    psum x1 -> x0, waiting for transfers between devices: 30.7 us -> none  [slot_factors(): row_sum = lax.psum(row_part, 'col')]
    dot_general x3, matrix products: 23.5 us -> 13.1 us  [slot_factors(): jnp.einsum('jw,wxab->jxab', placing, stacked, precision=lax.Precision.HIG...]
    reduce_sum x0 -> x3, other arithmetic: none -> 9.87 us  [slot_factors(): row_sum = jnp.sum(lax.all_gather(row_part, 'col'), axis=0)]
  transfers between devices with their start and end apart: 2 -> 4, of which waited for: 2 -> 3; matrix products, arithmetic and copies ran while one was open for 16% -> 29% of each run, Pallas kernels for 0% -> 0%
where the time goes in v1:
time: 628 us; the launch traced here: 618 us
  matrix products  244 us (39%)
  waiting for transfers between devices  239 us (38%)
  local copies, waits for them, and re-layouts  92.4 us (15%)
  other arithmetic  27.9 us (4%)
  between operations  14.7 us (2%)
    psum x1, waiting for transfers between devices, slot_factors(): received = lax.psum(slots, 'row')  175 us
    dot_general x12, matrix products, cols_update(): jnp.einsum('aibm,bml->aibl', matrix, factor, precision=lax.Precision.HIGH...  135 us
    dot_general x6, matrix products, rows_update(): jnp.einsum('aij,aibl->ajbl', factor, matrix, precision=lax.Precision.HIGH...  87.7 us
    all_gather x3, waiting for transfers between devices, slot_factors(): row_sum = jnp.sum(lax.all_gather(row_part, 'col'), axis=0)  64.3 us
    unnamed x36, local copies, waits for them, and re-layouts  41.7 us
    gather x3, local copies, waits for them, and re-layouts, window_bases(): jnp.take(factors[0], target, axis=0)  16.7 us
    gather x3, local copies, waits for them, and re-layouts, window_bases(): jnp.take(factors[1], target, axis=0)  16.6 us
    dot_general x3, matrix products, slot_factors(): jnp.einsum('jw,wxab->jxab', placing, stacked, precision=lax.Precision.HIG...  13.1 us
  transfers between devices with their start and end apart: 4, of which 3 were waited for; matrix products, arithmetic and copies ran while one was open for 29% of the time, Pallas kernels for 0%

profile of v1, /device:TPU:0, one launch (start us, length us, event | category | flops | bytes accessed | tf_op | source)
XLA Modules:
  0.0 618.0 jit_solution(15682667724849597643)
XLA Ops:
  12.0 6.4 %gather_fusion = f32[512,256]{1,0:T(8,128)} fusion(f32[2,256,256]{2,1,0:T(8,128)S(1)} %get-tuple-element.59, s32[512]{0:T(512)S(1)} %bitcast.242), kind=kCustom, calls=%fused_computation.clone | custom fusion | bytes 1052672 | tf_op jit(solution)/shard_map/vmap(jit(_take))/gather | solution.py:16
  18.4 6.4 %gather_fusion.1 = f32[512,256]{1,0:T(8,128)} fusion(f32[2,256,256]{2,1,0:T(8,128)S(1)} %get-tuple-element.60, s32[512]{0:T(512)S(1)} %bitcast.243), kind=kCustom, calls=%fused_computation.1.clone | custom fusion | bytes 1052672 | tf_op jit(solution)/shard_map/vmap(jit(_take))/gather | solution.py:16
  29.0 6.4 %gather_fusion.2 = f32[512,256]{1,0:T(8,128)} fusion(f32[2,256,256]{2,1,0:T(8,128)S(1)} %get-tuple-element.57, s32[512]{0:T(512)S(1)} %bitcast.246), kind=kCustom, calls=%fused_computation.2.clone | custom fusion | bytes 1052672 | tf_op jit(solution)/shard_map/vmap(jit(_take))/gather | solution.py:16
  35.3 6.4 %gather_fusion.3 = f32[512,256]{1,0:T(8,128)} fusion(f32[2,256,256]{2,1,0:T(8,128)S(1)} %get-tuple-element.58, s32[512]{0:T(512)S(1)} %bitcast.247), kind=kCustom, calls=%fused_computation.3.clone | custom fusion | bytes 1052672 | tf_op jit(solution)/shard_map/vmap(jit(_take))/gather | solution.py:16
  54.1 4.3 fusion.42
  63.9 4.6 fusion.50
  68.6 174.8 %all-reduce.3.cloned.1.call-done = (f32[8,2,256,256]{3,0,2,1:T(8,128)}, f32[8,2,256,256]{3,0,2,1:T(8,128)}, f32[8,2,256,256]{3,0,2,1:T(8,128)}) async-done(((f32[8,2,256,256]{3,0,2,1:T(8,128)}, f32[8,2,256,256]{3,0,2,1:T(8,128)}, f32[8,2,256,256]{3,0,2,1:T(8,128)}), (f32[8,2,256,256]{3,0,2,1:T(8,128)}, f32[8,2,256,256]{3,0,2,1:T(8,128)}, f32[8,2,256,256]{3,0,2,1:T(8,128)})) %all-reduce.3.cloned.1.call-update) | async-done | bytes 12582928 | tf_op jit(solution)/shard_map/psum | solution.py:38
  255.6 9.2 %fusion.31 = (f32[8,256,256,1]{2,0,1,3:T(8,128)}, f32[8,256,256,1]{2,0,1,3:T(8,128)}, f32[8,256,256,1]{2,0,1,3:T(8,128)}, f32[8,256,256,1]{2,0,1,3:T(8,128)S(1)}...) fusion(f32[8,2,256,256]{3,0,2,1:T(8,128)} %get-tuple-element.31, f32[256,256]{1,0:T(8,128)S(1)} %fusion.78, ...), kind=kLoop, calls=%fused_computation.41 | loop fusion | flops 4718592 | bytes 25428064 | tf_op jit(solution)/shard_map/add | solution.py:22
  264.8 21.2 %fusion.22 = f32[8,256,4,256]{3,1,2,0:T(8,128)} fusion(f32[4,256,8,256]{3,2,1,0:T(8,128)} %param.11, f32[8,256,256,1]{2,0,1,3:T(8,128)S(1)} %get-tuple-element.62), kind=kOutput, calls=%fused_computation.28 | convolution fusion | flops 6442450944 | bytes 18874368 | tf_op jit(solution)/shard_map/aibm,bml->aibl/dot_general | solution.py:30
  293.8 13.0 %fusion.6 = f32[8,256,4,256]{3,1,2,0:T(8,128)S(1)} fusion(f32[8,256,4,256]{3,1,2,0:T(8,128)} %fusion.22, f32[8,256,256,1]{2,0,1,3:T(8,128)} %get-tuple-element.64), kind=kOutput, calls=%fused_computation.12 | convolution fusion | flops 6442450944 | bytes 18874368 | tf_op jit(solution)/shard_map/aibm,bml->aibl/dot_general | solution.py:30
  306.8 10.2 %fusion.24 = f32[4,256,8,256]{1,3,0,2:T(8,128)} fusion(f32[8,256,4,256]{3,1,2,0:T(8,128)S(1)} %fusion.6, f32[8,256,256,1]{2,0,1,3:T(8,128)S(1)} %copy-done.5), kind=kOutput, calls=%fused_computation.30 | convolution fusion | flops 6442450944 | bytes 18874368 | tf_op jit(solution)/shard_map/aibm,bml->aibl/dot_general | solution.py:30
  317.0 10.4 %copy.226 = f32[4,256,8,256]{3,2,1,0:T(8,128)} copy(f32[4,256,8,256]{1,3,0,2:T(8,128)} %fusion.24) | data formatting | bytes 16777216
  327.4 15.0 %fusion.20 = f32[8,256,4,256]{3,1,2,0:T(8,128)S(1)} fusion(f32[8,256,256,1]{1,2,3,0:T(8,128)} %copy.234, f32[4,256,8,256]{3,2,1,0:T(8,128)} %param.12), kind=kOutput, calls=%fused_computation.26 | convolution fusion | flops 6442450944 | bytes 18874368 | tf_op jit(solution)/shard_map/aibm,bml->aibl/dot_general | solution.py:30
  342.4 8.8 %fusion.2 = f32[8,256,4,256]{3,1,2,0:T(8,128)S(1)} fusion(f32[8,256,256,1]{1,2,3,0:T(8,128)S(1)} %copy-done, f32[8,256,4,256]{3,1,2,0:T(8,128)S(1)} %fusion.20), kind=kOutput, calls=%fused_computation.8 | convolution fusion | flops 6442450944 | bytes 18874368 | tf_op jit(solution)/shard_map/aibm,bml->aibl/dot_general | solution.py:30
  351.3 10.1 %fusion.27 = f32[4,256,8,256]{1,3,0,2:T(8,128)} fusion(f32[8,256,256,1]{1,2,3,0:T(8,128)S(1)} %copy.241, f32[8,256,4,256]{3,1,2,0:T(8,128)S(1)} %fusion.2), kind=kOutput, calls=%fused_computation.31 | convolution fusion | flops 6442450944 | bytes 18874368 | tf_op jit(solution)/shard_map/aibm,bml->aibl/dot_general | solution.py:30
  361.3 10.4 %copy.227 = f32[4,256,8,256]{3,2,1,0:T(8,128)} copy(f32[4,256,8,256]{1,3,0,2:T(8,128)} %fusion.27) | data formatting | bytes 16777216
  374.4 34.7 %all-gather.9.cloned.1.call-done = f32[16,256,256]{2,1,0:T(8,128)} async-done(((f32[4,256,256]{2,1,0:T(8,128)}), f32[16,256,256]{2,1,0:T(8,128)}) %all-gather.9.cloned.1.call-update) | async-done | bytes 4194320 | tf_op jit(solution)/shard_map/all_gather | solution.py:41
  412.7 14.0 %fusion.18 = f32[4,256,8,256]{3,1,0,2:T(8,128)S(1)} fusion(f32[4,256,8,256]{3,2,1,0:T(8,128)} %param.9, f32[4,256,256]{2,1,0:T(8,128)S(1)} %reduce_sum.130, f32[4]{0:T(128)S(1)} %broadcast_subtract_fusion, f32[256,256]{1,0:T(8,128)S(1)} %fusion.78), kind=kOutput, calls=%fused_computation.24 | convolution fusion | flops 6442975232 | bytes 18087952 | tf_op jit(solution)/shard_map/aij,aibl->ajbl/dot_general | solution.py:26
  426.8 8.9 %fusion.117 = f32[8,256,4,256]{3,1,2,0:T(8,128)S(1)} fusion(f32[8,256,256,1]{1,2,3,0:T(8,128)S(1)} %copy-done.3, f32[4,256,8,256]{3,1,0,2:T(8,128)S(1)} %fusion.18), kind=kOutput, calls=%fused_computation.194 | convolution fusion | flops 6442450944 | bytes 18874368 | tf_op jit(solution)/shard_map/aibm,bml->aibl/dot_general | solution.py:30
  435.7 14.3 %fusion.16 = f32[4,256,8,256]{3,1,0,2:T(8,128)S(1)} fusion(f32[8,256,4,256]{3,1,2,0:T(8,128)S(1)} %fusion.117, f32[4,256,256]{2,1,0:T(8,128)S(1)} %copy-done.6, f32[4]{0:T(128)S(1)} %broadcast_subtract_fusion.1, f32[256,256]{1,0:T(8,128)S(1)} %fusion.78), kind=kOutput, calls=%fused_computation.22 | convolution fusion | flops 6442975232 | bytes 18087952 | tf_op jit(solution)/shard_map/aij,aibl->ajbl/dot_general | solution.py:26
  450.0 10.1 %fusion.118 = f32[8,256,4,256]{3,1,2,0:T(8,128)} fusion(f32[8,256,256,1]{1,2,3,0:T(8,128)S(1)} %copy-done.1, f32[4,256,8,256]{3,1,0,2:T(8,128)S(1)} %fusion.16), kind=kOutput, calls=%fused_computation.195 | convolution fusion | flops 6442450944 | bytes 18874368 | tf_op jit(solution)/shard_map/aibm,bml->aibl/dot_general | solution.py:30
  460.1 29.7 %all-gather.7.cloned.1.call-done = f32[16,256,256]{2,1,0:T(8,128)} async-done(((f32[4,256,256]{2,1,0:T(8,128)}), f32[16,256,256]{2,1,0:T(8,128)}) %all-gather.7.cloned.1.call-update) | async-done | bytes 4194320 | tf_op jit(solution)/shard_map/all_gather | solution.py:41
  493.3 16.6 %fusion.14 = f32[4,256,8,256]{3,1,0,2:T(8,128)S(1)} fusion(f32[8,256,4,256]{3,1,2,0:T(8,128)} %fusion.118, f32[4,256,256]{2,1,0:T(8,128)} %reduce_sum.122, f32[256,256]{1,0:T(8,128)S(1)} %fusion.78, f32[4]{0:T(128)S(1)} %broadcast_subtract_fusion.2), kind=kOutput, calls=%fused_computation.20 | convolution fusion | flops 6442975232 | bytes 18087952 | tf_op jit(solution)/shard_map/aij,aibl->ajbl/dot_general | solution.py:26
  509.9 9.9 %convolution_bitcast_fusion.1 = f32[4,256,8,256]{1,3,0,2:T(8,128)} fusion(f32[8,256,256,1]{1,2,3,0:T(8,128)S(1)} %copy.241, f32[4,256,8,256]{3,1,0,2:T(8,128)S(1)} %fusion.14), kind=kOutput, calls=%fused_computation.33 | convolution fusion | flops 6442450944 | bytes 18874368 | tf_op jit(solution)/shard_map/aibm,bml->aibl/dot_general | solution.py:30
  519.8 10.4 %copy.224 = f32[4,256,8,256]{3,2,1,0:T(8,128)} copy(f32[4,256,8,256]{1,3,0,2:T(8,128)} %convolution_bitcast_fusion.1) | data formatting | bytes 16777216
  530.2 14.0 %fusion.12 = f32[4,256,8,256]{3,1,0,2:T(8,128)S(1)} fusion(f32[4,256,8,256]{3,2,1,0:T(8,128)} %param.10, f32[4,256,256]{2,1,0:T(8,128)S(1)} %reduce_sum.130, f32[4]{0:T(128)S(1)} %broadcast_subtract_fusion, f32[256,256]{1,0:T(8,128)S(1)} %fusion.78), kind=kOutput, calls=%fused_computation.18 | convolution fusion | flops 6442975232 | bytes 18087952 | tf_op jit(solution)/shard_map/aij,aibl->ajbl/dot_general | solution.py:26
  544.2 8.9 %fusion.119 = f32[8,256,4,256]{3,1,2,0:T(8,128)S(1)} fusion(f32[8,256,256,1]{1,2,3,0:T(8,128)S(1)} %copy-done.4, f32[4,256,8,256]{3,1,0,2:T(8,128)S(1)} %fusion.12), kind=kOutput, calls=%fused_computation.196 | convolution fusion | flops 6442450944 | bytes 18874368 | tf_op jit(solution)/shard_map/aibm,bml->aibl/dot_general | solution.py:30
  553.2 14.5 %fusion.10 = f32[4,256,8,256]{3,1,0,2:T(8,128)S(1)} fusion(f32[8,256,4,256]{3,1,2,0:T(8,128)S(1)} %fusion.119, f32[4,256,256]{2,1,0:T(8,128)S(1)} %copy-done.7, f32[4]{0:T(128)S(1)} %broadcast_subtract_fusion.1, f32[256,256]{1,0:T(8,128)S(1)} %fusion.78), kind=kOutput, calls=%fused_computation.16 | convolution fusion | flops 6442975232 | bytes 18087952 | tf_op jit(solution)/shard_map/aij,aibl->ajbl/dot_general | solution.py:26
  567.7 9.0 %fusion.120 = f32[8,256,4,256]{3,1,2,0:T(8,128)S(1)} fusion(f32[8,256,256,1]{1,2,3,0:T(8,128)S(1)} %copy-done.2, f32[4,256,8,256]{3,1,0,2:T(8,128)S(1)} %fusion.10), kind=kOutput, calls=%fused_computation.197 | convolution fusion | flops 6442450944 | bytes 18874368 | tf_op jit(solution)/shard_map/aibm,bml->aibl/dot_general | solution.py:30
  576.7 14.3 %fusion.8 = f32[4,256,8,256]{3,1,0,2:T(8,128)S(1)} fusion(f32[8,256,4,256]{3,1,2,0:T(8,128)S(1)} %fusion.120, f32[4,256,256]{2,1,0:T(8,128)S(1)} %copy-done.8, f32[256,256]{1,0:T(8,128)S(1)} %fusion.78, f32[4]{0:T(128)S(1)} %broadcast_subtract_fusion.2), kind=kOutput, calls=%fused_computation.14 | convolution fusion | flops 6442975232 | bytes 18087952 | tf_op jit(solution)/shard_map/aij,aibl->ajbl/dot_general | solution.py:26
  591.0 9.7 %convolution_bitcast_fusion = f32[4,256,8,256]{1,3,0,2:T(8,128)} fusion(f32[8,256,256,1]{1,2,3,0:T(8,128)S(1)} %copy.241, f32[4,256,8,256]{3,1,0,2:T(8,128)S(1)} %fusion.8), kind=kOutput, calls=%fused_computation.32 | convolution fusion | flops 6442450944 | bytes 18874368 | tf_op jit(solution)/shard_map/aibm,bml->aibl/dot_general | solution.py:30
  600.7 10.4 %copy.225 = f32[4,256,8,256]{3,2,1,0:T(8,128)} copy(f32[4,256,8,256]{1,3,0,2:T(8,128)} %convolution_bitcast_fusion) | data formatting | bytes 16777216
  (104 shorter events, 56.6 us)
Async XLA Ops:
  7.2 3.3 copy-start.12
  7.2 236.2 %all-reduce.3.cloned.1.call-start = ((), (), s32[]{:S(2)}) async-start(), calls=%async_computation.3 | async-start | bytes 25165824 | tf_op jit(solution)/shard_map/psum | solution.py:38
  10.3 14.5 %copy-start.13 = (s32[3,16]{1,0:T(4,128)S(1)}, s32[3,16]{1,0:T(4,128)}, u32[]{:S(2)}) copy-start(s32[3,16]{1,0:T(4,128)} %param.13) | copy-start | bytes 580
  35.3 14.7 %copy-start.9 = (f32[512,256]{1,0:T(8,128)S(1)}, f32[512,256]{1,0:T(8,128)}, u32[]{:S(2)}) copy-start(f32[512,256]{1,0:T(8,128)} %gather_fusion) | copy-start | bytes 1572868
  35.3 14.7 %copy-start.10 = (f32[512,256]{1,0:T(8,128)S(1)}, f32[512,256]{1,0:T(8,128)}, u32[]{:S(2)}) copy-start(f32[512,256]{1,0:T(8,128)} %gather_fusion.1) | copy-start | bytes 1572868
  41.8 9.4 %copy-start.11 = (f32[512,256]{1,0:T(8,128)S(1)}, f32[512,256]{1,0:T(8,128)}, u32[]{:S(2)}) copy-start(f32[512,256]{1,0:T(8,128)} %gather_fusion.3) | copy-start | bytes 1572868
  68.5 303.2 %all-gather.11.cloned.1.call-start = ((), (), s32[]{:S(2)}) async-start(), calls=%async_computation.2 | async-start | bytes 5242880 | tf_op jit(solution)/shard_map/all_gather | solution.py:41
  247.2 161.8 %all-gather.9.cloned.1.call-start = ((), (), s32[]{:S(2)}) async-start(), calls=%async_computation.1 | async-start | bytes 5242880 | tf_op jit(solution)/shard_map/all_gather | solution.py:41
  251.2 238.6 %all-gather.7.cloned.1.call-start = ((), (), s32[]{:S(2)}) async-start(), calls=%async_computation | async-start | bytes 5242880 | tf_op jit(solution)/shard_map/all_gather | solution.py:41
  293.8 13.0 %copy-start.5 = (f32[8,256,256,1]{2,0,1,3:T(8,128)S(1)}, f32[8,256,256,1]{2,0,1,3:T(8,128)}, u32[]{:S(2)}) copy-start(f32[8,256,256,1]{2,0,1,3:T(8,128)} %get-tuple-element.46) | copy-start | bytes 6291460
  327.4 15.0 %copy-start = (f32[8,256,256,1]{1,2,3,0:T(8,128)S(1)}, f32[8,256,256,1]{1,2,3,0:T(8,128)}, u32[]{:S(2)}) copy-start(f32[8,256,256,1]{1,2,3,0:T(8,128)} %copy.238) | copy-start | bytes 6291460
  412.7 14.0 %copy-start.3 = (f32[8,256,256,1]{1,2,3,0:T(8,128)S(1)}, f32[8,256,256,1]{1,2,3,0:T(8,128)}, u32[]{:S(2)}) copy-start(f32[8,256,256,1]{1,2,3,0:T(8,128)} %copy.234) | copy-start | bytes 6291460
  426.8 8.9 %copy-start.6 = (f32[4,256,256]{2,1,0:T(8,128)S(1)}, f32[4,256,256]{2,1,0:T(8,128)}, u32[]{:S(2)}) copy-start(f32[4,256,256]{2,1,0:T(8,128)} %reduce_sum.126) | copy-start | bytes 3145732
  435.7 14.3 %copy-start.1 = (f32[8,256,256,1]{1,2,3,0:T(8,128)S(1)}, f32[8,256,256,1]{1,2,3,0:T(8,128)}, u32[]{:S(2)}) copy-start(f32[8,256,256,1]{1,2,3,0:T(8,128)} %copy.238) | copy-start | bytes 6291460
  530.2 14.1 %copy-start.4 = (f32[8,256,256,1]{1,2,3,0:T(8,128)S(1)}, f32[8,256,256,1]{1,2,3,0:T(8,128)}, u32[]{:S(2)}) copy-start(f32[8,256,256,1]{1,2,3,0:T(8,128)} %copy.234) | copy-start | bytes 6291460
  544.2 8.9 %copy-start.7 = (f32[4,256,256]{2,1,0:T(8,128)S(1)}, f32[4,256,256]{2,1,0:T(8,128)}, u32[]{:S(2)}) copy-start(f32[4,256,256]{2,1,0:T(8,128)} %reduce_sum.126) | copy-start | bytes 3145732
  553.1 14.5 %copy-start.2 = (f32[8,256,256,1]{1,2,3,0:T(8,128)S(1)}, f32[8,256,256,1]{1,2,3,0:T(8,128)}, u32[]{:S(2)}) copy-start(f32[8,256,256,1]{1,2,3,0:T(8,128)} %copy.238) | copy-start | bytes 6291460
  567.7 9.1 %copy-start.8 = (f32[4,256,256]{2,1,0:T(8,128)S(1)}, f32[4,256,256]{2,1,0:T(8,128)}, u32[]{:S(2)}) copy-start(f32[4,256,256]{2,1,0:T(8,128)} %reduce_sum.122) | copy-start | bytes 3145732
Sparse Core Ops, SparseCore 0:
  68.6 174.7 all-reduce.2
  247.4 80.8 all-gather.10
  329.8 79.2 all-gather.8
  410.5 79.2 all-gather.6
